TPU v7x, 32 devices: a whole 2x2x4 slice. The times are simulated.
32 devices in a mesh: groups: 2 (over y), blk: 4 (over z), rep: 4 (over x, core).
Axes of the slice: x: 2, y: 2, z: 4, core: 2. Of those that a mesh axis runs over, the one named last changes fastest.
Arguments:
- embeddings: float32 [8192, 128], P(('groups', 'blk')), parts along dimension 0, may hold values from -6 to 6
- degrees: int32 [8192], P(('groups', 'blk')), parts along dimension 0, may hold values from 1 to 12800, as said below
- tile_values: bfloat16 [8, 4, 1, 24, 128, 128], P(('groups', 'blk'), 'rep'), parts along dimension 0
- tile_rows: int32 [8, 4, 1, 24], P(('groups', 'blk'), 'rep'), parts along dimension 0, may hold values from 0 to 7
- tile_columns: int32 [8, 4, 1, 24], P(('groups', 'blk'), 'rep'), parts along dimension 0, may hold values from 0 to 7
- slot_counts: int32 [8, 4, 1], P(('groups', 'blk'), 'rep'), parts along dimension 0, may hold values from 6 to 24, as said below
Outputs:
- combined: float32 [8192, 128], P(('groups', 'blk', 'rep')), parts along dimension 0
There are 2 independent parts, one for each index of `groups`. A program takes and returns all parts, laid end to end along the dimension named above; each array names one. Nothing has to cross between parts.
Inputs may be any that keep to these rules, and one draw needn't show every extreme that they name: `degrees`: each node's degree is at least the number of nonzero entries in its row of A. `slot_counts`: some arc position of some device has all 24 slots live in every draw.
All inputs are finite; a program needn't handle non-finite values.
Results may differ from a plain program's by a relative error of at most 0.0003.
Values sent between devices are 32-bit elements; how exact they have to be, the bound alone decides.
A program may use at most 64 MiB of HBM per device.

v0:
```python
import jax
import jax.numpy as jnp
from jax import lax
from jax.sharding import PartitionSpec as P

LAYERS = 2


def shifted_2(shard, axis, by):
    devices = lax.axis_size(axis)
    return lax.ppermute(shard, axis, [(i, (i + by) % devices) for i in range(devices)])


def slot_term(source_panel, arc_slot, slots):
    tile_values, tile_rows, tile_columns, slot_counts = slots
    slot_total = tile_values.shape[1]
    block_total = source_panel.shape[0]
    columns = lax.dynamic_index_in_dim(tile_columns, arc_slot, 0, keepdims=False)
    values = lax.dynamic_index_in_dim(tile_values, arc_slot, 0, keepdims=False)
    row_blocks = lax.dynamic_index_in_dim(tile_rows, arc_slot, 0, keepdims=False)
    live_count = lax.dynamic_index_in_dim(slot_counts, arc_slot, 0, keepdims=False)
    blocks = jnp.take(source_panel, columns, axis=0)
    products = jnp.einsum(
        "jab,jbw->jaw",
        values,
        blocks,
        precision=lax.Precision.HIGHEST,
        preferred_element_type=jnp.float32,
    )
    live_slots = jnp.arange(slot_total, dtype=jnp.int32) < live_count
    placement = (
        (row_blocks[:, None] == jnp.arange(block_total, dtype=jnp.int32)[None, :])
        & live_slots[:, None]
    ).astype(jnp.float32)
    return jnp.einsum("jc,jaw->caw", placement, products, precision=lax.Precision.HIGHEST)


def arc_product(source_panel, slots, team_index, team_count):
    arc_length = slots[0].shape[0]
    arc_panel = source_panel
    for power_index in range(team_count.bit_length() - 1):
        shifted = shifted_2(arc_panel, "blk", arc_length * (1 << power_index))
        arc_panel = jnp.where(team_index >> power_index & 1 == 1, shifted, arc_panel)
    empty = jnp.zeros(source_panel.shape, jnp.float32)

    def walk(arc_slot, loop_state):
        partial_value, panel_now = loop_state
        partial_value = partial_value + slot_term(panel_now, arc_slot, slots)
        panel_now = shifted_2(panel_now, "blk", 1)
        return (partial_value, panel_now)

    partial_value, panel_now = lax.fori_loop(0, arc_length - 1, walk, (empty, arc_panel))
    return partial_value + slot_term(panel_now, arc_length - 1, slots)


def per_device(embeddings, degrees, tile_values, tile_rows, tile_columns, slot_counts):
    tile_size = tile_values.shape[-1]
    width_count = embeddings.shape[1]
    block_count = embeddings.shape[0] // tile_size
    slots = (tile_values[0, 0], tile_rows[0, 0], tile_columns[0, 0], slot_counts[0, 0])
    team_index = lax.axis_index("rep")
    team_count = lax.axis_size("rep")
    share_rows = embeddings.shape[0] // team_count
    norm_scale = lax.rsqrt(degrees.astype(jnp.float32))
    current = embeddings
    combined = lax.dynamic_slice_in_dim(embeddings, team_index * share_rows, share_rows)
    for layer_index in range(LAYERS):
        source_panel = (current * norm_scale[:, None]).reshape(block_count, tile_size, width_count)
        partial_value = arc_product(source_panel, slots, team_index, team_count)
        partial_value = partial_value.reshape(block_count * tile_size, width_count)
        current = lax.psum(partial_value, "rep") * norm_scale[:, None]
        combined = combined + lax.dynamic_slice_in_dim(current, team_index * share_rows, share_rows)
    return combined / (LAYERS + 1.0)


def solution(mesh):
    in_specs = (
        P(("groups", "blk"), None),
        P(("groups", "blk")),
        P(("groups", "blk"), "rep", None, None, None, None),
        P(("groups", "blk"), "rep", None, None),
        P(("groups", "blk"), "rep", None, None),
        P(("groups", "blk"), "rep", None),
    )
    out_specs = P(("groups", "blk", "rep"), None)
    return jax.shard_map(
        per_device, mesh=mesh, in_specs=in_specs, out_specs=out_specs, check_vma=False
    )
```

profile of v0, /device:TPU:0, one launch (start us, length us, event | category | flops | bytes accessed | tf_op | source)
XLA Modules:
  0.0 182.0 jit_solution(11972040666576285834)
XLA Ops:
  6.5 0.8 convert_rsqrt_fusion
  7.3 1.2 broadcast_multiply_fusion.2
  8.6 3.1 %collective-permute-start = (f32[8,128,128]{2,1,0:T(8,128)S(1)}, f32[8,128,128]{2,1,0:T(8,128)S(1)}, u32[]{:S(2)}, u32[]{:S(2)}) collective-permute-start(f32[8,128,128]{2,1,0:T(8,128)S(1)} %bitcast.28), channel_id=1, source_target_pairs={{0,4},{4,8},{8,12},{12,0},{1,5},{5,9},{9,13},{13,1},{2,6},{6,10},{... | collective-permute-start | bytes 1572872 | tf_op jit(solution)/shard_map/ppermute | solution.py:11
  12.3 13.3 %collective-permute-done = f32[8,128,128]{2,1,0:T(8,128)S(1)} collective-permute-done((f32[8,128,128]{2,1,0:T(8,128)S(1)}, f32[8,128,128]{2,1,0:T(8,128)S(1)}, u32[]{:S(2)}, u32[]{:S(2)}) %collective-permute-start) | collective-permute-done | bytes 524320 | tf_op jit(solution)/shard_map/ppermute | solution.py:11
  25.6 0.8 collective-permute-start.1
  26.5 23.3 %collective-permute-done.1 = f32[8,128,128]{2,1,0:T(8,128)S(1)} collective-permute-done((f32[8,128,128]{2,1,0:T(8,128)S(1)}, f32[8,128,128]{2,1,0:T(8,128)S(1)}, u32[]{:S(2)}, u32[]{:S(2)}) %collective-permute-start.1) | collective-permute-done | bytes 524320 | tf_op jit(solution)/shard_map/ppermute | solution.py:11
  49.9 1.8 gather_fusion
  51.7 2.9 %fusion.6 = f32[24,128,128]{2,1,0:T(8,128)S(1)} fusion(f32[24,128,128]{2,1,0:T(8,128)} %gather_fusion, bf16[1,1,1,24,128,128]{5,4,3,2,1,0:T(8,128)(2,1)S(1)} %copy-done, pred[24]{0:T(512)(128)(4,1)S(1)} %compare_and_fusion), kind=kOutput, calls=%fused_computation.8 | convolution fusion | flops 604372992 | bytes 3932184 | tf_op jit(solution)/shard_map/jab,jbw->jaw/dot_general | solution.py:23
  54.6 1.6 copy.9
  56.2 2.0 %fusion.2 = f32[8,128,128]{2,0,1:T(8,128)S(1)} fusion(f32[24,128,128]{1,0,2:T(8,128)} %copy.9, s32[24]{0:T(128)S(1)} %bitcast.32, pred[24]{0:T(512)(128)(4,1)S(1)} %iota_compare_fusion.1), kind=kOutput, calls=%fused_computation.4 | convolution fusion | flops 37749120 | bytes 2097272 | tf_op jit(solution)/shard_map/jc,jaw->caw/dot_general | solution.py:35
  58.2 0.9 copy.7
  59.2 33.4 %all-reduce.3.cloned.1.call-done = f32[1024,128]{1,0:T(8,128)} async-done(((f32[1024,128]{1,0:T(8,128)}), f32[1024,128]{1,0:T(8,128)}) %all-reduce.3.cloned.1.call-update) | async-done | bytes 524304 | tf_op jit(solution)/shard_map/psum | solution.py:71
  92.6 1.2 broadcast_multiply_fusion.1
  93.8 1.5 collective-permute-start.2
  95.4 12.8 %collective-permute-done.2 = f32[8,128,128]{2,1,0:T(8,128)S(1)} collective-permute-done((f32[8,128,128]{2,1,0:T(8,128)S(1)}, f32[8,128,128]{2,1,0:T(8,128)S(1)}, u32[]{:S(2)}, u32[]{:S(2)}) %collective-permute-start.2) | collective-permute-done | bytes 524320 | tf_op jit(solution)/shard_map/ppermute | solution.py:11
  108.3 0.9 collective-permute-start.3
  109.2 22.5 %collective-permute-done.3 = f32[8,128,128]{2,1,0:T(8,128)S(1)} collective-permute-done((f32[8,128,128]{2,1,0:T(8,128)S(1)}, f32[8,128,128]{2,1,0:T(8,128)S(1)}, u32[]{:S(2)}, u32[]{:S(2)}) %collective-permute-start.3) | collective-permute-done | bytes 524320 | tf_op jit(solution)/shard_map/ppermute | solution.py:11
  131.7 1.8 gather_fusion.1
  133.5 2.9 %fusion.4 = f32[24,128,128]{2,1,0:T(8,128)S(1)} fusion(f32[24,128,128]{2,1,0:T(8,128)} %gather_fusion.1, bf16[1,1,1,24,128,128]{5,4,3,2,1,0:T(8,128)(2,1)S(1)} %copy-done, pred[24]{0:T(512)(128)(4,1)S(1)} %compare_and_fusion), kind=kOutput, calls=%fused_computation.6 | convolution fusion | flops 604372992 | bytes 3932184 | tf_op jit(solution)/shard_map/jab,jbw->jaw/dot_general | solution.py:23
  136.4 1.6 copy.10
  138.0 2.0 %fusion = f32[8,128,128]{2,0,1:T(8,128)S(1)} fusion(f32[24,128,128]{1,0,2:T(8,128)} %copy.10, s32[24]{0:T(128)S(1)} %bitcast.33, pred[24]{0:T(512)(128)(4,1)S(1)} %iota_compare_fusion.1), kind=kOutput, calls=%fused_computation.2 | convolution fusion | flops 37749120 | bytes 2097272 | tf_op jit(solution)/shard_map/jc,jaw->caw/dot_general | solution.py:35
  140.1 0.9 copy.8
  141.1 32.4 %all-reduce.5.cloned.1.call-done = f32[1024,128]{1,0:T(8,128)} async-done(((f32[1024,128]{1,0:T(8,128)}), f32[1024,128]{1,0:T(8,128)}) %all-reduce.5.cloned.1.call-update) | async-done | bytes 524304 | tf_op jit(solution)/shard_map/psum | solution.py:71
  173.5 1.7 fusion.15
  (19 shorter events, 0.5 us)
Async XLA Ops:
  6.5 45.1 %copy-start = (bf16[1,1,1,24,128,128]{5,4,3,2,1,0:T(8,128)(2,1)S(1)}, bf16[1,1,1,24,128,128]{5,4,3,2,1,0:T(8,128)(2,1)}, u32[]{:S(2)}) copy-start(bf16[1,1,1,24,128,128]{5,4,3,2,1,0:T(8,128)(2,1)} %param.10) | copy-start | bytes 2359300
  6.5 19.9 %copy-start.2 = (s32[1,1,1,24]{3,2,1,0:T(1,128)S(1)}, s32[1,1,1,24]{3,2,1,0:T(1,128)}, u32[]{:S(2)}) copy-start(s32[1,1,1,24]{3,2,1,0:T(1,128)} %param.12) | copy-start | bytes 292
  6.5 86.1 %all-reduce.3.cloned.1.call-start = ((), (), s32[]{:S(2)}) async-start(), calls=%async_computation | async-start | bytes 1048576 | tf_op jit(solution)/shard_map/psum | solution.py:71
  8.6 17.0 %collective-permute-start = (f32[8,128,128]{2,1,0:T(8,128)S(1)}, f32[8,128,128]{2,1,0:T(8,128)S(1)}, u32[]{:S(2)}, u32[]{:S(2)}) collective-permute-start(f32[8,128,128]{2,1,0:T(8,128)S(1)} %bitcast.28), channel_id=1, source_target_pairs={{0,4},{4,8},{8,12},{12,0},{1,5},{5,9},{9,13},{13,1},{2,6},{6,10},{... | collective-permute-start | bytes 1572872 | tf_op jit(solution)/shard_map/ppermute | solution.py:11
  25.6 24.1 %collective-permute-start.1 = (f32[8,128,128]{2,1,0:T(8,128)S(1)}, f32[8,128,128]{2,1,0:T(8,128)S(1)}, u32[]{:S(2)}, u32[]{:S(2)}) collective-permute-start(f32[8,128,128]{2,1,0:T(8,128)S(1)} %broadcast_select_fusion.1), channel_id=1, source_target_pairs={{0,8},{4,12},{8,0},{12,4},{1,9},{5,13},{9,1},{13,5},{2,10},{6,14},... | collective-permute-start | bytes 1572872 | tf_op jit(solution)/shard_map/ppermute | solution.py:11
  54.5 1.6 copy-start.1
  59.1 114.3 %all-reduce.5.cloned.1.call-start = ((), (), s32[]{:S(2)}) async-start(), calls=%async_computation.1 | async-start | bytes 1048576 | tf_op jit(solution)/shard_map/psum | solution.py:71
  93.8 14.4 %collective-permute-start.2 = (f32[8,128,128]{2,1,0:T(8,128)S(1)}, f32[8,128,128]{2,1,0:T(8,128)S(1)}, u32[]{:S(2)}, u32[]{:S(2)}) collective-permute-start(f32[8,128,128]{2,1,0:T(8,128)S(1)} %bitcast.26), channel_id=1, source_target_pairs={{0,4},{4,8},{8,12},{12,0},{1,5},{5,9},{9,13},{13,1},{2,6},{6,10},{... | collective-permute-start | bytes 1572872 | tf_op jit(solution)/shard_map/ppermute | solution.py:11
  108.3 23.3 %collective-permute-start.3 = (f32[8,128,128]{2,1,0:T(8,128)S(1)}, f32[8,128,128]{2,1,0:T(8,128)S(1)}, u32[]{:S(2)}, u32[]{:S(2)}) collective-permute-start(f32[8,128,128]{2,1,0:T(8,128)S(1)} %broadcast_select_fusion), channel_id=1, source_target_pairs={{0,8},{4,12},{8,0},{12,4},{1,9},{5,13},{9,1},{13,5},{2,10},{6,14},... | collective-permute-start | bytes 1572872 | tf_op jit(solution)/shard_map/ppermute | solution.py:11
Sparse Core Ops, SparseCore 0:
  59.3 33.2 all-reduce.2
  141.1 32.3 all-reduce.4
where the time goes:
time: 182 us
  waiting for transfers between devices  138 us (76%)
  between operations  14.1 us (8%)
  matrix products  9.86 us (5%)
  local copies, waits for them, and re-layouts  8.72 us (5%)
  starting transfers between devices  6.33 us (3%)
  other arithmetic  5.26 us (3%)
    ppermute x4, waiting for transfers between devices, shifted_2(): lax.ppermute(shard, axis, [(i, (i + by) % devices) for i in range(devices)])  71.9 us
    psum x2, waiting for transfers between devices, per_device(): current = lax.psum(partial_value, 'rep') * norm_scale[:, None]  65.8 us
    ppermute x4, starting transfers between devices, shifted_2(): lax.ppermute(shard, axis, [(i, (i + by) % devices) for i in range(devices)])  6.29 us
    dot_general x2, matrix products, slot_term(): jnp.einsum('jab,jbw->jaw', values, blocks, precision=lax.Precision.HIGHES...  5.78 us
    dot_general x2, matrix products, slot_term(): jnp.einsum('jc,jaw->caw', placement, products, precision=lax.Precision.HI...  4.08 us
  transfers between devices with their start and end apart: 6, of which 6 were waited for; matrix products, arithmetic and copies ran while one was open for 0% of the time, Pallas kernels for 0%

commit v1 on v0

--- a/solution.py
+++ b/solution.py
@@ -1,9 +1,14 @@
+import functools
+
 import jax
 import jax.numpy as jnp
 from jax import lax
+from jax.experimental import pallas as pl
+from jax.experimental.pallas import tpu as pltpu
 from jax.sharding import PartitionSpec as P
 
 LAYERS = 2
+MESH = pl.DeviceIdType.MESH
 
 
 def shifted_2(shard, axis, by):
@@ -73,6 +78,253 @@
     return combined / (LAYERS + 1.0)
 
 
+def team_kernel(
+    teams, emb_hbm, deg_ref, tiles_hbm, rows_ref, cols_ref, counts_ref, out_ref,
+    emb_own, norm_own, tiles, running, running_hi, running_lo, keys, a_hi, a_lo,
+    x_send, x_recv, x_pair, p_send, p_recv,
+    local_sems, x_send_sems, x_recv_sems, p_send_sems, p_recv_sems,
+):
+    z = lax.axis_index("blk")
+    r = lax.axis_index("rep")
+    slots, tile_size, width = tiles.shape[0], tiles.shape[1], emb_own.shape[1]
+    share = emb_own.shape[0]
+    side = a_hi.shape[0] // tile_size
+    blocks_own = share // tile_size
+
+    load_emb = pltpu.make_async_copy(
+        emb_hbm.at[pl.ds(pl.multiple_of(r * share, share), share)], emb_own, local_sems.at[0]
+    )
+    load_tiles = pltpu.make_async_copy(tiles_hbm, tiles, local_sems.at[1])
+    load_emb.start()
+    load_tiles.start()
+
+    barrier = pltpu.get_barrier_semaphore()
+    for dz in range(teams):
+        for dr in range(teams):
+            if dz or dr:
+                pl.semaphore_signal(
+                    barrier,
+                    inc=1,
+                    device_id={"blk": lax.rem(z + dz, teams), "rep": lax.rem(r + dr, teams)},
+                    device_id_type=MESH,
+                )
+
+    for i in range(blocks_own):
+        scale_row = lax.rsqrt(deg_ref[r * blocks_own + i].astype(jnp.float32))
+        norm_own[i * tile_size : (i + 1) * tile_size] = jnp.broadcast_to(
+            scale_row, (width, tile_size)
+        ).T
+    load_emb.wait()
+    x_send[0] = emb_own[...] * norm_own[...]
+    pl.semaphore_wait(barrier, teams * teams - 1)
+
+    def x_copy(layer, team):
+        return pltpu.make_async_remote_copy(
+            src_ref=x_send.at[layer],
+            dst_ref=x_recv.at[layer, r],
+            send_sem=x_send_sems.at[layer, team],
+            recv_sem=x_recv_sems.at[layer, r],
+            device_id={"blk": lax.rem(z + team, teams), "rep": team},
+            device_id_type=MESH,
+        )
+
+    def x_arrival(layer, quarter):
+        return pltpu.make_async_remote_copy(
+            src_ref=x_send.at[layer],
+            dst_ref=x_recv.at[layer, quarter],
+            send_sem=x_send_sems.at[layer, quarter],
+            recv_sem=x_recv_sems.at[layer, quarter],
+            device_id={"blk": lax.rem(z + 1, teams), "rep": r},
+            device_id_type=MESH,
+        )
+
+    def send_x(layer):
+        for team in (2, 3, 1):
+            x_copy(layer, team).start()
+
+        @pl.when(r != 0)
+        def _():
+            x_copy(layer, 0).start()
+
+        @pl.when(r == 0)
+        def _():
+            x_recv[layer, 0] = x_send[layer]
+
+    def take_x(layer):
+        for quarter in (1, 2, 3, 0):
+            if quarter == 0:
+                @pl.when(r != 0)
+                def _():
+                    x_arrival(layer, 0).wait_recv()
+            else:
+                x_arrival(layer, quarter).wait_recv()
+            value = x_recv[layer, quarter]
+            high = value.astype(jnp.bfloat16)
+            low = (value - high.astype(jnp.float32)).astype(jnp.bfloat16)
+            x_pair[quarter * share : (quarter + 1) * share, :width] = high
+            x_pair[quarter * share : (quarter + 1) * share, width:] = low
+
+    def build():
+        live = counts_ref[0]
+        for j in range(slots):
+            keys[j] = jnp.where(j < live, rows_ref[j] * side + cols_ref[j], side * side)
+        running[0] = jnp.zeros((tile_size, tile_size), jnp.float32)
+        running_hi[0] = jnp.zeros((tile_size, tile_size), jnp.bfloat16)
+        running_lo[0] = jnp.zeros((tile_size, tile_size), jnp.bfloat16)
+        load_tiles.wait()
+
+        def accumulate(j, carry):
+            own_key = keys[j]
+            before = jnp.int32(0)
+            for i in range(slots):
+                before = jnp.where((keys[i] == own_key) & (i < j), i + 1, before)
+            total = running[before] + tiles[j].astype(jnp.float32)
+            high = total.astype(jnp.bfloat16)
+            running[j + 1] = total
+            running_hi[j + 1] = high
+            running_lo[j + 1] = (total - high.astype(jnp.float32)).astype(jnp.bfloat16)
+            return carry
+
+        lax.fori_loop(0, slots, accumulate, 0)
+
+        def place(row, carry):
+            start = pl.multiple_of(row * tile_size, tile_size)
+            for column in range(side):
+                last = jnp.int32(0)
+                for j in range(slots):
+                    last = jnp.where(keys[j] == row * side + column, j + 1, last)
+                span = slice(column * tile_size, (column + 1) * tile_size)
+                a_hi[pl.ds(start, tile_size), span] = running_hi[last]
+                a_lo[pl.ds(start, tile_size), span] = running_lo[last]
+            return carry
+
+        lax.fori_loop(0, side, place, 0)
+
+    def product(part):
+        start = pl.multiple_of(part * share, share)
+        both = jnp.dot(
+            a_hi[pl.ds(start, share), :], x_pair[...], preferred_element_type=jnp.float32
+        )
+        rest = jnp.dot(
+            a_lo[pl.ds(start, share), :], x_pair[:, :width], preferred_element_type=jnp.float32
+        )
+        return both[:, :width] + (both[:, width:] + rest)
+
+    chip, core = r // 2, r % 2
+    partners = (2 * (1 - chip) + core, 2 * (1 - chip) + (1 - core), 2 * chip + (1 - core))
+
+    def p_copy(layer, turn):
+        return pltpu.make_async_remote_copy(
+            src_ref=p_send.at[layer, turn],
+            dst_ref=p_recv.at[layer, turn],
+            send_sem=p_send_sems.at[layer, turn],
+            recv_sem=p_recv_sems.at[layer, turn],
+            device_id={"blk": z, "rep": partners[turn]},
+            device_id_type=MESH,
+        )
+
+    send_x(0)
+    build()
+    combined = None
+    for layer in range(LAYERS):
+        take_x(layer)
+        for turn in range(teams - 1):
+            p_send[layer, turn] = product(partners[turn])
+            p_copy(layer, turn).start()
+        total = product(r)
+        for turn in (2, 0, 1):
+            p_copy(layer, turn).wait_recv()
+            total = total + p_recv[layer, turn]
+        current = total * norm_own[...]
+        if layer < LAYERS - 1:
+            x_send[layer + 1] = current * norm_own[...]
+            send_x(layer + 1)
+        if layer == 0:
+            emb_own[...] = emb_own[...] + current
+        else:
+            out_ref[...] = (emb_own[...] + current) / (LAYERS + 1.0)
+
+    for layer in range(LAYERS):
+        for team in range(1, teams):
+            x_copy(layer, team).wait_send()
+
+        @pl.when(r != 0)
+        def _():
+            x_copy(layer, 0).wait_send()
+
+        for turn in range(teams - 1):
+            p_copy(layer, turn).wait_send()
+
+
+def per_device_fused(embeddings, degrees, tile_values, tile_rows, tile_columns, slot_counts):
+    teams = lax.axis_size("rep")
+    slots, tile_size = tile_values.shape[3], tile_values.shape[-1]
+    nodes, width = embeddings.shape
+    share = nodes // teams
+    f32, bf16 = jnp.float32, jnp.bfloat16
+    smem = pl.BlockSpec(memory_space=pltpu.SMEM)
+    vmem = pl.BlockSpec(memory_space=pltpu.VMEM)
+    hbm = pl.BlockSpec(memory_space=pl.ANY)
+    dma = pltpu.SemaphoreType.DMA
+    return pl.pallas_call(
+        functools.partial(team_kernel, teams),
+        name="team_propagate",
+        out_shape=jax.ShapeDtypeStruct((share, width), f32),
+        in_specs=[hbm, vmem, hbm, smem, smem, smem],
+        out_specs=vmem,
+        scratch_shapes=[
+            pltpu.VMEM((share, width), f32),
+            pltpu.VMEM((share, width), f32),
+            pltpu.VMEM((slots, tile_size, tile_size), bf16),
+            pltpu.VMEM((slots + 1, tile_size, tile_size), f32),
+            pltpu.VMEM((slots + 1, tile_size, tile_size), bf16),
+            pltpu.VMEM((slots + 1, tile_size, tile_size), bf16),
+            pltpu.SMEM((slots,), jnp.int32),
+            pltpu.VMEM((nodes, nodes), bf16),
+            pltpu.VMEM((nodes, nodes), bf16),
+            pltpu.VMEM((LAYERS, share, width), f32),
+            pltpu.VMEM((LAYERS, teams, share, width), f32),
+            pltpu.VMEM((nodes, 2 * width), bf16),
+            pltpu.VMEM((LAYERS, teams - 1, share, width), f32),
+            pltpu.VMEM((LAYERS, teams - 1, share, width), f32),
+            dma((2,)),
+            dma((LAYERS, teams)),
+            dma((LAYERS, teams)),
+            dma((LAYERS, teams - 1)),
+            dma((LAYERS, teams - 1)),
+        ],
+        compiler_params=pltpu.CompilerParams(
+            collective_id=0, has_side_effects=True, vmem_limit_bytes=40 * 1024 * 1024
+        ),
+    )(
+        embeddings,
+        degrees.reshape(nodes // tile_size, 1, tile_size),
+        tile_values.reshape(slots, tile_size, tile_size),
+        tile_rows.reshape(slots),
+        tile_columns.reshape(slots),
+        slot_counts.reshape(1),
+    )
+
+
+def program_for(mesh):
+    teams, cycle = mesh.shape["rep"], mesh.shape["blk"]
+
+    def run(embeddings, degrees, tile_values, tile_rows, tile_columns, slot_counts):
+        nodes, tile_size = embeddings.shape[0], tile_values.shape[-1]
+        fits = (
+            teams == 4
+            and cycle == 4
+            and tile_values.shape[2] == 1
+            and nodes % (teams * tile_size) == 0
+            and nodes <= 1024
+            and embeddings.shape[1] == tile_size == 128
+        )
+        form = per_device_fused if fits else per_device
+        return form(embeddings, degrees, tile_values, tile_rows, tile_columns, slot_counts)
+
+    return run
+
+
 def solution(mesh):
     in_specs = (
         P(("groups", "blk"), None),
@@ -84,5 +336,5 @@
     )
     out_specs = P(("groups", "blk", "rep"), None)
     return jax.shard_map(
-        per_device, mesh=mesh, in_specs=in_specs, out_specs=out_specs, check_vma=False
-    )
+        program_for(mesh), mesh=mesh, in_specs=in_specs, out_specs=out_specs, check_vma=False
+    )

time: 182 us -> 45.7 us (0.25)
  the two profiles are of different devices: /device:TPU:0 before, /device:TPU:12 now
where the time goes in v1:
time: 45.7 us; the launch traced here: 45.5 us
  Pallas kernels  41.3 us (90%)
  local copies, waits for them, and re-layouts  3.5 us (8%)
  between operations  0.69 us (2%)
    pallas_call x1, Pallas kernels, per_device_fused(): pl.pallas_call(functools.partial(team_kernel, teams), name='team_propagat...  41.3 us
    unnamed x11, local copies, waits for them, and re-layouts  3.5 us

profile of v1, /device:TPU:12, one launch (start us, length us, event | category | flops | bytes accessed | tf_op | source)
XLA Modules:
  0.0 45.5 jit_solution(12910875114678598330)
XLA Ops:
  0.7 0.0 copy-start.2
  0.7 0.0 copy-start.3
  0.7 0.0 copy-start.4
  0.7 0.7 %copy-done.2 = s32[1024]{0:T(1024)S(1)} copy-done((s32[1024]{0:T(1024)S(1)}, s32[1024]{0:T(1024)}, u32[]{:S(2)}) %copy-start.2) | copy-done | bytes 4120
  1.3 0.0 copy-done.3
  1.3 0.0 copy-done.4
  1.3 0.0 copy-start
  1.3 1.1 %copy-done = bf16[1,1,1,24,128,128]{5,4,3,2,1,0:T(8,128)(2,1)S(1)} copy-done((bf16[1,1,1,24,128,128]{5,4,3,2,1,0:T(8,128)(2,1)S(1)}, bf16[1,1,1,24,128,128]{5,4,3,2,1,0:T(8,128)(2,1)}, u32[]{:S(2)}) %copy-start) | copy-done | bytes 786456
  2.5 0.0 copy-start.1
  2.5 1.0 %copy-done.1 = f32[1024,128]{1,0:T(8,128)S(1)} copy-done((f32[1024,128]{1,0:T(8,128)S(1)}, f32[1024,128]{1,0:T(8,128)}, u32[]{:S(2)}) %copy-start.1) | copy-done | bytes 524312
  3.5 41.3 %team_propagate.1 = f32[256,128]{1,0:T(8,128)S(1)} custom-call(f32[1024,128]{1,0:T(8,128)S(1)} %copy-done.1, s32[8,1,128]{2,1,0:T(1,128)S(1)} %bitcast.7, bf16[24,128,128]{2,1,0:T(8,128)(2,1)S(1)} %bitcast.6, s32[24]{0:T(128)S(1)} %bitcast.8, s32[24]{0:T(128)S(1)} %bitcast.9, s32[1]{0:T(128)} %bitcast.5.counts_ref), custom_call_target="tpu_custom_call" | custom-call | tf_op jit(solution)/shard_map/team_propagate/pallas_call | solution.py:269
  44.8 0.7 %copy.9 = f32[256,128]{1,0:T(8,128)} copy(f32[256,128]{1,0:T(8,128)S(1)} %team_propagate.1) | data formatting | bytes 262144
Async XLA Ops:
  0.7 0.7 %copy-start.2 = (s32[1024]{0:T(1024)S(1)}, s32[1024]{0:T(1024)}, u32[]{:S(2)}) copy-start(s32[1024]{0:T(1024)} %param.7) | copy-start | bytes 12292
  0.7 0.7 %copy-start.3 = (s32[1,1,1,24]{3,2,1,0:T(1,128)S(1)}, s32[1,1,1,24]{3,2,1,0:T(1,128)}, u32[]{:S(2)}) copy-start(s32[1,1,1,24]{3,2,1,0:T(1,128)} %param.9) | copy-start | bytes 292
  0.7 0.7 %copy-start.4 = (s32[1,1,1,24]{3,2,1,0:T(1,128)S(1)}, s32[1,1,1,24]{3,2,1,0:T(1,128)}, u32[]{:S(2)}) copy-start(s32[1,1,1,24]{3,2,1,0:T(1,128)} %param.10) | copy-start | bytes 292
  1.3 1.1 %copy-start = (bf16[1,1,1,24,128,128]{5,4,3,2,1,0:T(8,128)(2,1)S(1)}, bf16[1,1,1,24,128,128]{5,4,3,2,1,0:T(8,128)(2,1)}, u32[]{:S(2)}) copy-start(bf16[1,1,1,24,128,128]{5,4,3,2,1,0:T(8,128)(2,1)} %param.8) | copy-start | bytes 2359300
  2.5 1.0 %copy-start.1 = (f32[1024,128]{1,0:T(8,128)S(1)}, f32[1024,128]{1,0:T(8,128)}, u32[]{:S(2)}) copy-start(f32[1024,128]{1,0:T(8,128)} %emb_hbm.1) | copy-start | bytes 1572868

commit v2 on v1

--- a/solution.py
+++ b/solution.py
@@ -79,99 +79,136 @@
 
 
 def team_kernel(
-    teams, emb_hbm, deg_ref, tiles_hbm, rows_ref, cols_ref, counts_ref, out_ref,
-    emb_own, norm_own, tiles, running, running_hi, running_lo, keys, a_hi, a_lo,
-    x_send, x_recv, x_pair, p_send, p_recv,
-    local_sems, x_send_sems, x_recv_sems, p_send_sems, p_recv_sems,
+    teams, chunks, emb_hbm, deg_hbm, tiles_hbm, rows_hbm, cols_hbm, counts_hbm, out_ref,
+    emb_own, norm_own, deg_own, tiles, running, running_hi, running_lo,
+    rows_ref, cols_ref, counts_ref, keys, a_hi, a_lo,
+    x_send, x_recv, x_pair, pair_send, pair_recv, mine, cross_send, cross_recv,
+    local_sems, x_send_sems, x_recv_sems, pair_send_sems, pair_recv_sems,
+    cross_send_sems, cross_recv_sems,
 ):
     z = lax.axis_index("blk")
     r = lax.axis_index("rep")
+    chip, core = r // 2, r % 2
+    sibling, opposite = 2 * chip + (1 - core), 2 * (1 - chip) + core
     slots, tile_size, width = tiles.shape[0], tiles.shape[1], emb_own.shape[1]
     share = emb_own.shape[0]
+    piece = share // chunks
     side = a_hi.shape[0] // tile_size
     blocks_own = share // tile_size
 
-    load_emb = pltpu.make_async_copy(
-        emb_hbm.at[pl.ds(pl.multiple_of(r * share, share), share)], emb_own, local_sems.at[0]
-    )
-    load_tiles = pltpu.make_async_copy(tiles_hbm, tiles, local_sems.at[1])
-    load_emb.start()
-    load_tiles.start()
+    loads = [
+        pltpu.make_async_copy(source, target, local_sems.at[i])
+        for i, (source, target) in enumerate(
+            (
+                (deg_hbm.at[pl.ds(r * blocks_own, blocks_own)], deg_own),
+                (emb_hbm.at[pl.ds(pl.multiple_of(r * share, share), share)], emb_own),
+                (rows_hbm, rows_ref),
+                (cols_hbm, cols_ref),
+                (counts_hbm, counts_ref),
+                (tiles_hbm, tiles),
+            )
+        )
+    ]
+    for load in loads:
+        load.start()
 
     barrier = pltpu.get_barrier_semaphore()
-    for dz in range(teams):
-        for dr in range(teams):
-            if dz or dr:
-                pl.semaphore_signal(
-                    barrier,
-                    inc=1,
-                    device_id={"blk": lax.rem(z + dz, teams), "rep": lax.rem(r + dr, teams)},
-                    device_id_type=MESH,
-                )
-
+
+    def greet(shard, team):
+        pl.semaphore_signal(
+            barrier,
+            inc=1,
+            device_id={"blk": lax.rem(shard, teams), "rep": lax.rem(team, teams)},
+            device_id_type=MESH,
+        )
+
+    for step in range(1, teams):
+        greet(z + step, jnp.int32(step))
+        greet(z, r + step)
+
+    @pl.when(r != 0)
+    def _():
+        for quarter in range(teams):
+            greet(z + teams - r, jnp.int32(quarter))
+
+    loads[0].wait()
     for i in range(blocks_own):
-        scale_row = lax.rsqrt(deg_ref[r * blocks_own + i].astype(jnp.float32))
+        scale_row = lax.rsqrt(deg_own[i].astype(jnp.float32))
         norm_own[i * tile_size : (i + 1) * tile_size] = jnp.broadcast_to(
             scale_row, (width, tile_size)
         ).T
-    load_emb.wait()
+    loads[1].wait()
     x_send[0] = emb_own[...] * norm_own[...]
-    pl.semaphore_wait(barrier, teams * teams - 1)
-
-    def x_copy(layer, team):
+
+    @pl.when(r == 0)
+    def _():
+        pl.semaphore_wait(barrier, 2 * (teams - 1))
+
+    @pl.when(r != 0)
+    def _():
+        pl.semaphore_wait(barrier, 3 * teams - 2)
+
+    def x_copy(layer, chunk, team):
+        rows = pl.ds(chunk * piece, piece)
         return pltpu.make_async_remote_copy(
-            src_ref=x_send.at[layer],
-            dst_ref=x_recv.at[layer, r],
-            send_sem=x_send_sems.at[layer, team],
-            recv_sem=x_recv_sems.at[layer, r],
+            src_ref=x_send.at[layer, rows],
+            dst_ref=x_recv.at[layer, r, rows],
+            send_sem=x_send_sems.at[layer, chunk, team],
+            recv_sem=x_recv_sems.at[layer, chunk, r],
             device_id={"blk": lax.rem(z + team, teams), "rep": team},
             device_id_type=MESH,
         )
 
-    def x_arrival(layer, quarter):
+    def x_arrival(layer, chunk, quarter):
+        rows = pl.ds(chunk * piece, piece)
         return pltpu.make_async_remote_copy(
-            src_ref=x_send.at[layer],
-            dst_ref=x_recv.at[layer, quarter],
-            send_sem=x_send_sems.at[layer, quarter],
-            recv_sem=x_recv_sems.at[layer, quarter],
+            src_ref=x_send.at[layer, rows],
+            dst_ref=x_recv.at[layer, quarter, rows],
+            send_sem=x_send_sems.at[layer, chunk, quarter],
+            recv_sem=x_recv_sems.at[layer, chunk, quarter],
             device_id={"blk": lax.rem(z + 1, teams), "rep": r},
             device_id_type=MESH,
         )
 
-    def send_x(layer):
+    def send_x(layer, chunk):
         for team in (2, 3, 1):
-            x_copy(layer, team).start()
+            x_copy(layer, chunk, team).start()
 
         @pl.when(r != 0)
         def _():
-            x_copy(layer, 0).start()
+            x_copy(layer, chunk, 0).start()
 
         @pl.when(r == 0)
         def _():
-            x_recv[layer, 0] = x_send[layer]
+            rows = pl.ds(chunk * piece, piece)
+            x_recv[layer, 0, rows] = x_send[layer, rows]
 
     def take_x(layer):
-        for quarter in (1, 2, 3, 0):
-            if quarter == 0:
-                @pl.when(r != 0)
-                def _():
-                    x_arrival(layer, 0).wait_recv()
-            else:
-                x_arrival(layer, quarter).wait_recv()
-            value = x_recv[layer, quarter]
-            high = value.astype(jnp.bfloat16)
-            low = (value - high.astype(jnp.float32)).astype(jnp.bfloat16)
-            x_pair[quarter * share : (quarter + 1) * share, :width] = high
-            x_pair[quarter * share : (quarter + 1) * share, width:] = low
+        for chunk in range(chunks):
+            for quarter in range(teams):
+                if quarter == 0:
+                    @pl.when(r != 0)
+                    def _():
+                        x_arrival(layer, chunk, 0).wait_recv()
+                else:
+                    x_arrival(layer, chunk, quarter).wait_recv()
+                value = x_recv[layer, quarter, pl.ds(chunk * piece, piece)]
+                high = value.astype(jnp.bfloat16)
+                low = (value - high.astype(jnp.float32)).astype(jnp.bfloat16)
+                first = quarter * share + chunk * piece
+                x_pair[first : first + piece, :width] = high
+                x_pair[first : first + piece, width:] = low
 
     def build():
-        live = counts_ref[0]
+        for load in loads[2:5]:
+            load.wait()
+        live = counts_ref[0, 0, 0]
         for j in range(slots):
             keys[j] = jnp.where(j < live, rows_ref[j] * side + cols_ref[j], side * side)
         running[0] = jnp.zeros((tile_size, tile_size), jnp.float32)
         running_hi[0] = jnp.zeros((tile_size, tile_size), jnp.bfloat16)
         running_lo[0] = jnp.zeros((tile_size, tile_size), jnp.bfloat16)
-        load_tiles.wait()
+        loads[5].wait()
 
         def accumulate(j, carry):
             own_key = keys[j]
@@ -200,101 +237,127 @@
 
         lax.fori_loop(0, side, place, 0)
 
-    def product(part):
-        start = pl.multiple_of(part * share, share)
+    def product(part, chunk):
+        start = pl.multiple_of(part * share + chunk * piece, piece)
         both = jnp.dot(
-            a_hi[pl.ds(start, share), :], x_pair[...], preferred_element_type=jnp.float32
+            a_hi[pl.ds(start, piece), :], x_pair[...], preferred_element_type=jnp.float32
         )
         rest = jnp.dot(
-            a_lo[pl.ds(start, share), :], x_pair[:, :width], preferred_element_type=jnp.float32
+            a_lo[pl.ds(start, piece), :], x_pair[:, :width], preferred_element_type=jnp.float32
         )
         return both[:, :width] + (both[:, width:] + rest)
 
-    chip, core = r // 2, r % 2
-    partners = (2 * (1 - chip) + core, 2 * (1 - chip) + (1 - core), 2 * chip + (1 - core))
-
-    def p_copy(layer, turn):
+    def neighbour_copy(source, target, send_sems, recv_sems, layer, chunk, team):
         return pltpu.make_async_remote_copy(
-            src_ref=p_send.at[layer, turn],
-            dst_ref=p_recv.at[layer, turn],
-            send_sem=p_send_sems.at[layer, turn],
-            recv_sem=p_recv_sems.at[layer, turn],
-            device_id={"blk": z, "rep": partners[turn]},
+            src_ref=source.at[layer, chunk],
+            dst_ref=target.at[layer, chunk],
+            send_sem=send_sems.at[layer, chunk],
+            recv_sem=recv_sems.at[layer, chunk],
+            device_id={"blk": z, "rep": team},
             device_id_type=MESH,
         )
 
-    send_x(0)
+    def pair_copy(layer, chunk):
+        return neighbour_copy(
+            pair_send, pair_recv, pair_send_sems, pair_recv_sems, layer, chunk, sibling
+        )
+
+    def cross_copy(layer, chunk):
+        return neighbour_copy(
+            cross_send, cross_recv, cross_send_sems, cross_recv_sems, layer, chunk, opposite
+        )
+
+    for chunk in range(chunks):
+        send_x(0, chunk)
     build()
-    combined = None
     for layer in range(LAYERS):
         take_x(layer)
-        for turn in range(teams - 1):
-            p_send[layer, turn] = product(partners[turn])
-            p_copy(layer, turn).start()
-        total = product(r)
-        for turn in (2, 0, 1):
-            p_copy(layer, turn).wait_recv()
-            total = total + p_recv[layer, turn]
-        current = total * norm_own[...]
-        if layer < LAYERS - 1:
-            x_send[layer + 1] = current * norm_own[...]
-            send_x(layer + 1)
-        if layer == 0:
-            emb_own[...] = emb_own[...] + current
-        else:
-            out_ref[...] = (emb_own[...] + current) / (LAYERS + 1.0)
+        for chunk in range(chunks):
+            pair_send[layer, chunk, 0] = product(2 * (1 - chip) + (1 - core), chunk)
+            pair_send[layer, chunk, 1] = product(sibling, chunk)
+            pair_copy(layer, chunk).start()
+            mine[chunk, 0] = product(opposite, chunk)
+            mine[chunk, 1] = product(r, chunk)
+            if chunk > 0:
+                pair_copy(layer, chunk - 1).wait_recv()
+                cross_send[layer, chunk - 1] = mine[chunk - 1, 0] + pair_recv[layer, chunk - 1, 0]
+                cross_copy(layer, chunk - 1).start()
+        pair_copy(layer, chunks - 1).wait_recv()
+        cross_send[layer, chunks - 1] = mine[chunks - 1, 0] + pair_recv[layer, chunks - 1, 0]
+        cross_copy(layer, chunks - 1).start()
+        for chunk in range(chunks):
+            rows = pl.ds(chunk * piece, piece)
+            cross_copy(layer, chunk).wait_recv()
+            total = (mine[chunk, 1] + pair_recv[layer, chunk, 1]) + cross_recv[layer, chunk]
+            current = total * norm_own[rows]
+            if layer < LAYERS - 1:
+                x_send[layer + 1, rows] = current * norm_own[rows]
+                send_x(layer + 1, chunk)
+                emb_own[rows] = emb_own[rows] + current
+            else:
+                out_ref[rows] = (emb_own[rows] + current) / (LAYERS + 1.0)
 
     for layer in range(LAYERS):
-        for team in range(1, teams):
-            x_copy(layer, team).wait_send()
-
-        @pl.when(r != 0)
-        def _():
-            x_copy(layer, 0).wait_send()
-
-        for turn in range(teams - 1):
-            p_copy(layer, turn).wait_send()
+        for chunk in range(chunks):
+            for team in range(1, teams):
+                x_copy(layer, chunk, team).wait_send()
+
+            @pl.when(r != 0)
+            def _():
+                x_copy(layer, chunk, 0).wait_send()
+
+            pair_copy(layer, chunk).wait_send()
+            cross_copy(layer, chunk).wait_send()
 
 
 def per_device_fused(embeddings, degrees, tile_values, tile_rows, tile_columns, slot_counts):
     teams = lax.axis_size("rep")
+    chunks = 2
     slots, tile_size = tile_values.shape[3], tile_values.shape[-1]
     nodes, width = embeddings.shape
     share = nodes // teams
-    f32, bf16 = jnp.float32, jnp.bfloat16
-    smem = pl.BlockSpec(memory_space=pltpu.SMEM)
-    vmem = pl.BlockSpec(memory_space=pltpu.VMEM)
-    hbm = pl.BlockSpec(memory_space=pl.ANY)
+    piece = share // chunks
+    f32, bf16, i32 = jnp.float32, jnp.bfloat16, jnp.int32
+    hbm = pl.BlockSpec(memory_space=pltpu.HBM)
     dma = pltpu.SemaphoreType.DMA
     return pl.pallas_call(
-        functools.partial(team_kernel, teams),
+        functools.partial(team_kernel, teams, chunks),
         name="team_propagate",
         out_shape=jax.ShapeDtypeStruct((share, width), f32),
-        in_specs=[hbm, vmem, hbm, smem, smem, smem],
-        out_specs=vmem,
+        in_specs=[hbm] * 6,
+        out_specs=pl.BlockSpec(memory_space=pltpu.VMEM),
         scratch_shapes=[
             pltpu.VMEM((share, width), f32),
             pltpu.VMEM((share, width), f32),
+            pltpu.VMEM((share // tile_size, 1, tile_size), i32),
             pltpu.VMEM((slots, tile_size, tile_size), bf16),
             pltpu.VMEM((slots + 1, tile_size, tile_size), f32),
             pltpu.VMEM((slots + 1, tile_size, tile_size), bf16),
             pltpu.VMEM((slots + 1, tile_size, tile_size), bf16),
-            pltpu.SMEM((slots,), jnp.int32),
+            pltpu.SMEM((slots,), i32),
+            pltpu.SMEM((slots,), i32),
+            pltpu.SMEM((1, 1, 1), i32),
+            pltpu.SMEM((slots,), i32),
             pltpu.VMEM((nodes, nodes), bf16),
             pltpu.VMEM((nodes, nodes), bf16),
             pltpu.VMEM((LAYERS, share, width), f32),
             pltpu.VMEM((LAYERS, teams, share, width), f32),
             pltpu.VMEM((nodes, 2 * width), bf16),
-            pltpu.VMEM((LAYERS, teams - 1, share, width), f32),
-            pltpu.VMEM((LAYERS, teams - 1, share, width), f32),
-            dma((2,)),
-            dma((LAYERS, teams)),
-            dma((LAYERS, teams)),
-            dma((LAYERS, teams - 1)),
-            dma((LAYERS, teams - 1)),
+            pltpu.VMEM((LAYERS, chunks, 2, piece, width), f32),
+            pltpu.VMEM((LAYERS, chunks, 2, piece, width), f32),
+            pltpu.VMEM((chunks, 2, piece, width), f32),
+            pltpu.VMEM((LAYERS, chunks, piece, width), f32),
+            pltpu.VMEM((LAYERS, chunks, piece, width), f32),
+            dma((6,)),
+            dma((LAYERS, chunks, teams)),
+            dma((LAYERS, chunks, teams)),
+            dma((LAYERS, chunks)),
+            dma((LAYERS, chunks)),
+            dma((LAYERS, chunks)),
+            dma((LAYERS, chunks)),
         ],
         compiler_params=pltpu.CompilerParams(
-            collective_id=0, has_side_effects=True, vmem_limit_bytes=40 * 1024 * 1024
+            collective_id=0, has_side_effects=True, vmem_limit_bytes=64 * 1024 * 1024
         ),
     )(
         embeddings,
@@ -302,7 +365,7 @@
         tile_values.reshape(slots, tile_size, tile_size),
         tile_rows.reshape(slots),
         tile_columns.reshape(slots),
-        slot_counts.reshape(1),
+        slot_counts,
     )
 
 

time: 45.7 us -> 44.9 us (0.982)
  the two profiles are of different devices: /device:TPU:12 before, /device:TPU:0 now
where the time goes in v2:
time: 44.9 us; the launch traced here: 44.8 us
  Pallas kernels  42.6 us (95%)
  local copies, waits for them, and re-layouts  1.57 us (3%)
  between operations  0.66 us (1%)
    pallas_call x1, Pallas kernels, per_device_fused(): pl.pallas_call(functools.partial(team_kernel, teams, chunks), name='team_...  42.6 us
    unnamed x1, local copies, waits for them, and re-layouts  1.57 us

profile of v2, /device:TPU:0, one launch (start us, length us, event | category | flops | bytes accessed | tf_op | source)
XLA Modules:
  0.0 44.8 jit_solution(3100305370862876349)
XLA Ops:
  0.7 42.6 %team_propagate.1 = f32[256,128]{1,0:T(8,128)} custom-call(f32[1024,128]{1,0:T(8,128)} %emb_hbm.1, s32[8,1,128]{2,1,0:T(1,128)} %bitcast.5, bf16[24,128,128]{2,1,0:T(8,128)(2,1)} %bitcast.4, s32[24]{0:T(128)} %bitcast.6, s32[24]{0:T(128)} %bitcast.7, s32[1,1,1]{2,1,0:T(1,128)S(6)} %copy.8.counts_hbm), custom_call_target="tpu_custom_call" | custom-call | tf_op jit(solution)/shard_map/team_propagate/pallas_call | solution.py:323
  43.2 1.6 %copy.9 = f32[256,128]{1,0:T(8,128)} copy(f32[256,128]{1,0:T(8,128)} %team_propagate.1) | data formatting | bytes 262144

commit v3 on v2

--- a/solution.py
+++ b/solution.py
@@ -79,10 +79,10 @@
 
 
 def team_kernel(
-    teams, chunks, emb_hbm, deg_hbm, tiles_hbm, rows_hbm, cols_hbm, counts_hbm, out_ref,
+    teams, x_chunks, emb_hbm, deg_hbm, tiles_hbm, rows_hbm, cols_hbm, counts_hbm, out_ref,
     emb_own, norm_own, deg_own, tiles, running, running_hi, running_lo,
     rows_ref, cols_ref, counts_ref, keys, a_hi, a_lo,
-    x_send, x_recv, x_pair, pair_send, pair_recv, mine, cross_send, cross_recv,
+    x_send, x_recv, x_pair, pair_send, pair_recv, cross_send, cross_recv,
     local_sems, x_send_sems, x_recv_sems, pair_send_sems, pair_recv_sems,
     cross_send_sems, cross_recv_sems,
 ):
@@ -92,7 +92,7 @@
     sibling, opposite = 2 * chip + (1 - core), 2 * (1 - chip) + core
     slots, tile_size, width = tiles.shape[0], tiles.shape[1], emb_own.shape[1]
     share = emb_own.shape[0]
-    piece = share // chunks
+    x_piece = share // x_chunks
     side = a_hi.shape[0] // tile_size
     blocks_own = share // tile_size
 
@@ -149,7 +149,7 @@
         pl.semaphore_wait(barrier, 3 * teams - 2)
 
     def x_copy(layer, chunk, team):
-        rows = pl.ds(chunk * piece, piece)
+        rows = pl.ds(chunk * x_piece, x_piece)
         return pltpu.make_async_remote_copy(
             src_ref=x_send.at[layer, rows],
             dst_ref=x_recv.at[layer, r, rows],
@@ -160,7 +160,7 @@
         )
 
     def x_arrival(layer, chunk, quarter):
-        rows = pl.ds(chunk * piece, piece)
+        rows = pl.ds(chunk * x_piece, x_piece)
         return pltpu.make_async_remote_copy(
             src_ref=x_send.at[layer, rows],
             dst_ref=x_recv.at[layer, quarter, rows],
@@ -180,24 +180,23 @@
 
         @pl.when(r == 0)
         def _():
-            rows = pl.ds(chunk * piece, piece)
+            rows = pl.ds(chunk * x_piece, x_piece)
             x_recv[layer, 0, rows] = x_send[layer, rows]
 
-    def take_x(layer):
-        for chunk in range(chunks):
-            for quarter in range(teams):
-                if quarter == 0:
-                    @pl.when(r != 0)
-                    def _():
-                        x_arrival(layer, chunk, 0).wait_recv()
-                else:
-                    x_arrival(layer, chunk, quarter).wait_recv()
-                value = x_recv[layer, quarter, pl.ds(chunk * piece, piece)]
-                high = value.astype(jnp.bfloat16)
-                low = (value - high.astype(jnp.float32)).astype(jnp.bfloat16)
-                first = quarter * share + chunk * piece
-                x_pair[first : first + piece, :width] = high
-                x_pair[first : first + piece, width:] = low
+    def take_x(layer, chunk):
+        for quarter in range(teams):
+            if quarter == 0:
+                @pl.when(r != 0)
+                def _():
+                    x_arrival(layer, chunk, 0).wait_recv()
+            else:
+                x_arrival(layer, chunk, quarter).wait_recv()
+            value = x_recv[layer, quarter, pl.ds(chunk * x_piece, x_piece)]
+            high = value.astype(jnp.bfloat16)
+            low = (value - high.astype(jnp.float32)).astype(jnp.bfloat16)
+            first = (chunk * teams + quarter) * x_piece
+            x_pair[first : first + x_piece, :width] = high
+            x_pair[first : first + x_piece, width:] = low
 
     def build():
         for load in loads[2:5]:
@@ -237,13 +236,13 @@
 
         lax.fori_loop(0, side, place, 0)
 
-    def product(part, chunk):
-        start = pl.multiple_of(part * share + chunk * piece, piece)
+    def product(part):
+        start = pl.multiple_of(part * share, share)
         both = jnp.dot(
-            a_hi[pl.ds(start, piece), :], x_pair[...], preferred_element_type=jnp.float32
+            a_hi[pl.ds(start, share), :], x_pair[...], preferred_element_type=jnp.float32
         )
         rest = jnp.dot(
-            a_lo[pl.ds(start, piece), :], x_pair[:, :width], preferred_element_type=jnp.float32
+            a_lo[pl.ds(start, share), :], x_pair[:, :width], preferred_element_type=jnp.float32
         )
         return both[:, :width] + (both[:, width:] + rest)
 
@@ -267,38 +266,35 @@
             cross_send, cross_recv, cross_send_sems, cross_recv_sems, layer, chunk, opposite
         )
 
-    for chunk in range(chunks):
+    for chunk in range(x_chunks):
         send_x(0, chunk)
     build()
     for layer in range(LAYERS):
-        take_x(layer)
-        for chunk in range(chunks):
-            pair_send[layer, chunk, 0] = product(2 * (1 - chip) + (1 - core), chunk)
-            pair_send[layer, chunk, 1] = product(sibling, chunk)
-            pair_copy(layer, chunk).start()
-            mine[chunk, 0] = product(opposite, chunk)
-            mine[chunk, 1] = product(r, chunk)
-            if chunk > 0:
-                pair_copy(layer, chunk - 1).wait_recv()
-                cross_send[layer, chunk - 1] = mine[chunk - 1, 0] + pair_recv[layer, chunk - 1, 0]
-                cross_copy(layer, chunk - 1).start()
-        pair_copy(layer, chunks - 1).wait_recv()
-        cross_send[layer, chunks - 1] = mine[chunks - 1, 0] + pair_recv[layer, chunks - 1, 0]
-        cross_copy(layer, chunks - 1).start()
-        for chunk in range(chunks):
-            rows = pl.ds(chunk * piece, piece)
-            cross_copy(layer, chunk).wait_recv()
-            total = (mine[chunk, 1] + pair_recv[layer, chunk, 1]) + cross_recv[layer, chunk]
-            current = total * norm_own[rows]
-            if layer < LAYERS - 1:
-                x_send[layer + 1, rows] = current * norm_own[rows]
+        for chunk in range(x_chunks):
+            take_x(layer, chunk)
+        pair_send[layer, 0] = product(2 * (1 - chip) + (1 - core))
+        pair_copy(layer, 0).start()
+        for_opposite = product(opposite)
+        pair_copy(layer, 0).wait_recv()
+        cross_send[layer, 0] = for_opposite + pair_recv[layer, 0]
+        cross_copy(layer, 0).start()
+        pair_send[layer, 1] = product(sibling)
+        pair_copy(layer, 1).start()
+        total = product(r)
+        pair_copy(layer, 1).wait_recv()
+        total = total + pair_recv[layer, 1]
+        cross_copy(layer, 0).wait_recv()
+        current = (total + cross_recv[layer, 0]) * norm_own[...]
+        if layer < LAYERS - 1:
+            x_send[layer + 1] = current * norm_own[...]
+            for chunk in range(x_chunks):
                 send_x(layer + 1, chunk)
-                emb_own[rows] = emb_own[rows] + current
-            else:
-                out_ref[rows] = (emb_own[rows] + current) / (LAYERS + 1.0)
+            emb_own[...] = emb_own[...] + current
+        else:
+            out_ref[...] = (emb_own[...] + current) / (LAYERS + 1.0)
 
     for layer in range(LAYERS):
-        for chunk in range(chunks):
+        for chunk in range(x_chunks):
             for team in range(1, teams):
                 x_copy(layer, chunk, team).wait_send()
 
@@ -306,22 +302,22 @@
             def _():
                 x_copy(layer, chunk, 0).wait_send()
 
-            pair_copy(layer, chunk).wait_send()
-            cross_copy(layer, chunk).wait_send()
+        pair_copy(layer, 0).wait_send()
+        pair_copy(layer, 1).wait_send()
+        cross_copy(layer, 0).wait_send()
 
 
 def per_device_fused(embeddings, degrees, tile_values, tile_rows, tile_columns, slot_counts):
     teams = lax.axis_size("rep")
-    chunks = 2
+    x_chunks = 1
     slots, tile_size = tile_values.shape[3], tile_values.shape[-1]
     nodes, width = embeddings.shape
     share = nodes // teams
-    piece = share // chunks
     f32, bf16, i32 = jnp.float32, jnp.bfloat16, jnp.int32
     hbm = pl.BlockSpec(memory_space=pltpu.HBM)
     dma = pltpu.SemaphoreType.DMA
     return pl.pallas_call(
-        functools.partial(team_kernel, teams, chunks),
+        functools.partial(team_kernel, teams, x_chunks),
         name="team_propagate",
         out_shape=jax.ShapeDtypeStruct((share, width), f32),
         in_specs=[hbm] * 6,
@@ -343,18 +339,17 @@
             pltpu.VMEM((LAYERS, share, width), f32),
             pltpu.VMEM((LAYERS, teams, share, width), f32),
             pltpu.VMEM((nodes, 2 * width), bf16),
-            pltpu.VMEM((LAYERS, chunks, 2, piece, width), f32),
-            pltpu.VMEM((LAYERS, chunks, 2, piece, width), f32),
-            pltpu.VMEM((chunks, 2, piece, width), f32),
-            pltpu.VMEM((LAYERS, chunks, piece, width), f32),
-            pltpu.VMEM((LAYERS, chunks, piece, width), f32),
+            pltpu.VMEM((LAYERS, 2, share, width), f32),
+            pltpu.VMEM((LAYERS, 2, share, width), f32),
+            pltpu.VMEM((LAYERS, 1, share, width), f32),
+            pltpu.VMEM((LAYERS, 1, share, width), f32),
             dma((6,)),
-            dma((LAYERS, chunks, teams)),
-            dma((LAYERS, chunks, teams)),
-            dma((LAYERS, chunks)),
-            dma((LAYERS, chunks)),
-            dma((LAYERS, chunks)),
-            dma((LAYERS, chunks)),
+            dma((LAYERS, x_chunks, teams)),
+            dma((LAYERS, x_chunks, teams)),
+            dma((LAYERS, 2)),
+            dma((LAYERS, 2)),
+            dma((LAYERS, 1)),
+            dma((LAYERS, 1)),
         ],
         compiler_params=pltpu.CompilerParams(
             collective_id=0, has_side_effects=True, vmem_limit_bytes=64 * 1024 * 1024

time: 44.9 us -> 42.8 us (0.953)
  Pallas kernels: 42.6 us -> 40.4 us
    pallas_call x1, Pallas kernels: 42.6 us -> 40.4 us  [per_device_fused(): pl.pallas_call(functools.partial(team_kernel, teams, x_chunks), name='tea...]
where the time goes in v3:
time: 42.8 us; the launch traced here: 42.6 us
  Pallas kernels  40.4 us (94%)
  local copies, waits for them, and re-layouts  1.57 us (4%)
  between operations  0.66 us (2%)
    pallas_call x1, Pallas kernels, per_device_fused(): pl.pallas_call(functools.partial(team_kernel, teams, x_chunks), name='tea...  40.4 us
    unnamed x1, local copies, waits for them, and re-layouts  1.57 us

profile of v3, /device:TPU:0, one launch (start us, length us, event | category | flops | bytes accessed | tf_op | source)
XLA Modules:
  0.0 42.6 jit_solution(1993727152660510066)
XLA Ops:
  0.7 40.4 %team_propagate.1 = f32[256,128]{1,0:T(8,128)} custom-call(f32[1024,128]{1,0:T(8,128)} %emb_hbm.1, s32[8,1,128]{2,1,0:T(1,128)} %bitcast.5, bf16[24,128,128]{2,1,0:T(8,128)(2,1)} %bitcast.4, s32[24]{0:T(128)} %bitcast.6, s32[24]{0:T(128)} %bitcast.7, s32[1,1,1]{2,1,0:T(1,128)S(6)} %copy.8.counts_hbm), custom_call_target="tpu_custom_call" | custom-call | tf_op jit(solution)/shard_map/team_propagate/pallas_call | solution.py:319
  41.1 1.6 %copy.9 = f32[256,128]{1,0:T(8,128)} copy(f32[256,128]{1,0:T(8,128)} %team_propagate.1) | data formatting | bytes 262144
